TPU v7x, 512 devices: a whole 4x4x16 slice. The times are simulated.
512 devices in a mesh: dp: 32 (over y, x, core), seq: 16 (over z).
Axes of the slice: x: 4, y: 4, z: 16, core: 2. Of those that a mesh axis runs over, the one named last changes fastest.
Arguments:
- queries: bfloat16 [32, 2048, 2048], P('dp', 'seq')
- keys: bfloat16 [32, 2048, 2048], P('dp', 'seq')
- events: bfloat16 [32, 2048, 2048], P('dp', 'seq'), may hold values from -6 to 6
- out_grad: bfloat16 [32, 2048, 2048], P('dp', 'seq'), may hold values from -6 to 6
- segment_ids: int32 [32, 2048], P('dp', 'seq'), may hold values from 0 to 63, never falling along the last dimension, each value on 1 to 512 neighbouring positions
- block_list: int32 [32, 16, 4], P('dp'), may hold values from 0 to 15, as said below
- conv_weight: float32 [64, 2048], replicated, may hold values from -0.75 to 0.75
Outputs:
- query_grad: bfloat16 [32, 2048, 2048], P('dp', 'seq')
- key_grad: bfloat16 [32, 2048, 2048], P('dp', 'seq')
- event_grad: bfloat16 [32, 2048, 2048], P('dp', 'seq')
- filter_grad: float32 [64, 2048], replicated
Inputs may be any that keep to these rules, and one draw needn't show every extreme that they name: `block_list`: entry 0 for query block b is b itself; every entry for block b lies in 0 .. b; entries may repeat.
All inputs are finite; a program needn't handle non-finite values.
Results may differ from a plain program's by a relative error of at most 0.015.
Values may be sent and summed in bfloat16 or wider, within the bound.
A program may use at most 64 MiB of HBM per device.

v0:
```python
import jax
import jax.numpy as jnp
from jax import lax
from jax.sharding import PartitionSpec as P

HD = 64
BLOCK = 128


def shifted(value, axis, steps):
    count = lax.axis_size(axis)
    initial, last = (max(0, -steps), min(count, count - steps))
    return lax.ppermute(value, axis, [(source, source + steps) for source in range(initial, last)])


def contract(form, left, right, exact):
    if exact:
        return jnp.einsum(
            form, left, right, precision=lax.Precision.HIGHEST, preferred_element_type=jnp.float32
        )
    return jnp.einsum(form, left, right, preferred_element_type=jnp.float32)


def causal_conv(padded, ids_ext, weight, count):
    taps = weight.shape[0]
    own = ids_ext[taps - 1 : taps - 1 + count]
    total = jnp.zeros((count, padded.shape[1]), jnp.float32)
    for step in range(taps):
        begin = taps - 1 - step
        piece = padded[begin : begin + count].astype(jnp.float32)
        match = (ids_ext[begin : begin + count] == own)[:, None]
        total = total + jnp.where(match, piece * weight[step : step + 1], 0.0)
    return total


def anti_conv(padded, ids_ext, weight, count):
    taps = weight.shape[0]
    own = ids_ext[0:count]
    total = jnp.zeros((count, padded.shape[1]), jnp.float32)
    for step in range(taps):
        piece = padded[step : step + count].astype(jnp.float32)
        match = (ids_ext[step : step + count] == own)[:, None]
        total = total + jnp.where(match, piece * weight[step : step + 1], 0.0)
    return total


def tap_gradient(grad, padded, ids_ext, taps):
    count = grad.shape[0]
    own = ids_ext[taps - 1 : taps - 1 + count]
    grad_wide = grad.astype(jnp.float32)
    sums = []
    for step in range(taps):
        begin = taps - 1 - step
        piece = padded[begin : begin + count].astype(jnp.float32)
        match = (ids_ext[begin : begin + count] == own)[:, None]
        sums.append(jnp.sum(jnp.where(match, piece * grad_wide, 0.0), axis=0))
    return jnp.stack(sums, axis=0)


def block_attention(query, key_rows, value, grad, ids, blist, block):
    tokens, head_dim = query.shape
    nblk = tokens // block
    nsel = blist.shape[1]
    scale = head_dim ** (-0.5)
    same = blist[:, :, None] == blist[:, None, :]
    before = jnp.arange(nsel)[None, :, None] > jnp.arange(nsel)[None, None, :]
    fresh = jnp.logical_not(jnp.any(same & before, axis=2))
    chosen = (blist[:, :, None] == jnp.arange(nblk, dtype=jnp.int32)[None, None, :]) & fresh[
        :, :, None
    ]
    picker = chosen.astype(jnp.bfloat16)
    q_blk = query.reshape(nblk, block, head_dim)
    k_blk = key_rows.reshape(nblk, block, head_dim)
    v_blk = value.reshape(nblk, block, head_dim)
    g_blk = grad.reshape(nblk, block, head_dim)
    k_sel = contract("bjc,cmd->bjmd", picker, k_blk, False).astype(jnp.bfloat16)
    v_sel = contract("bjc,cmd->bjmd", picker, v_blk, False).astype(jnp.bfloat16)
    id_blk = ids.reshape(nblk, block)
    id_sel = jnp.sum(jnp.where(chosen[:, :, :, None], id_blk[None, None, :, :], 0), axis=2)
    q_pos = (
        jnp.arange(nblk, dtype=jnp.int32)[:, None] * block
        + jnp.arange(block, dtype=jnp.int32)[None, :]
    )
    k_pos = blist[:, :, None] * block + jnp.arange(block, dtype=jnp.int32)[None, None, :]
    allowed = (
        fresh[:, None, :, None]
        & (k_pos[:, None] <= q_pos[:, :, None, None])
        & (id_sel[:, None] == id_blk[:, :, None, None])
    )
    scores = contract("bid,bjmd->bijm", q_blk, k_sel, False) * scale
    scores = jnp.where(allowed, scores, -1e30)
    top = jnp.max(scores, axis=(2, 3), keepdims=True)
    weights = jnp.where(allowed, jnp.exp(scores - top), 0.0)
    probs = weights / jnp.sum(weights, axis=(2, 3), keepdims=True)
    probs_low = probs.astype(jnp.bfloat16)
    attended = contract("bijm,bjmd->bid", probs_low, v_sel, False)
    delta = jnp.sum(g_blk.astype(jnp.float32) * attended, axis=2)
    dprobs = contract("bid,bjmd->bijm", g_blk, v_sel, False)
    dscores = (probs * (dprobs - delta[:, :, None, None])).astype(jnp.bfloat16)
    q_grad = (contract("bijm,bjmd->bid", dscores, k_sel, False) * scale).astype(jnp.bfloat16)
    k_slot = contract("bijm,bid->bjmd", dscores, q_blk, False) * scale
    v_slot = contract("bijm,bid->bjmd", probs_low, g_blk, False)
    spread = chosen.astype(jnp.float32)
    k_grad = contract("bjc,bjmd->cmd", spread, k_slot, True).astype(jnp.bfloat16)
    v_grad = contract("bjc,bjmd->cmd", spread, v_slot, True).astype(jnp.bfloat16)
    return (
        q_grad.reshape(tokens, head_dim),
        k_grad.reshape(tokens, head_dim),
        v_grad.reshape(tokens, head_dim),
    )


def heads_attention(query, key_rows, value, grad, ids, blist, head_dim, block):
    tokens, width = query.shape
    heads = width // head_dim

    def split(array):
        return array.reshape(tokens, heads, head_dim).transpose(1, 0, 2)

    def join(array):
        return array.transpose(1, 0, 2).reshape(tokens, width)

    def one_head(item):
        return block_attention(item[0], item[1], item[2], item[3], ids, blist, block)

    q_grad, k_grad, v_grad = lax.map(
        one_head, (split(query), split(key_rows), split(value), split(grad))
    )
    return (join(q_grad), join(k_grad), join(v_grad))


def per_device(queries, keys, events, out_grad, segment_ids, block_list, conv_weight):
    query = queries[0]
    key_rows = keys[0]
    feats = events[0]
    grad = out_grad[0]
    blist = block_list[0]
    rows, width = query.shape
    taps = conv_weight.shape[0]
    shards = lax.axis_size("dp") * lax.axis_size("seq")
    position = lax.axis_index("seq")
    all_ids = lax.all_gather(segment_ids, "seq", axis=1, tiled=True)[0]
    rim = jnp.zeros((taps - 1,), jnp.int32)
    ids_all = jnp.concatenate([rim, all_ids + 1, rim])
    left_ids = lax.dynamic_slice_in_dim(ids_all, position * rows, rows + taps - 1, 0)
    right_ids = lax.dynamic_slice_in_dim(ids_all, position * rows + taps - 1, rows + taps - 1, 0)
    earlier = shifted(feats[rows - (taps - 1) :], "seq", 1)
    padded = jnp.concatenate([earlier, feats], axis=0)
    values = causal_conv(padded, left_ids, conv_weight, rows).astype(jnp.bfloat16)
    head_q, head_k, head_v, head_g = (
        lax.all_to_all(query, "seq", split_axis=1, concat_axis=0, tiled=True),
        lax.all_to_all(key_rows, "seq", split_axis=1, concat_axis=0, tiled=True),
        lax.all_to_all(values, "seq", split_axis=1, concat_axis=0, tiled=True),
        lax.all_to_all(grad, "seq", split_axis=1, concat_axis=0, tiled=True),
    )
    q_grad, k_grad, v_grad = heads_attention(
        head_q, head_k, head_v, head_g, all_ids, blist, HD, BLOCK
    )
    q_back, k_back, v_back = (
        lax.all_to_all(q_grad, "seq", split_axis=0, concat_axis=1, tiled=True),
        lax.all_to_all(k_grad, "seq", split_axis=0, concat_axis=1, tiled=True),
        lax.all_to_all(v_grad, "seq", split_axis=0, concat_axis=1, tiled=True),
    )
    later = shifted(v_back[: taps - 1], "seq", -1)
    after = jnp.concatenate([v_back, later], axis=0)
    e_grad = anti_conv(after, right_ids, conv_weight, rows).astype(jnp.bfloat16)
    f_local = tap_gradient(v_back, padded, left_ids, taps)
    f_grad = lax.psum(f_local, ("dp", "seq")) / shards
    return (q_back[None], k_back[None], e_grad[None], f_grad)


def solution(mesh):
    in_specs = (
        P("dp", "seq", None),
        P("dp", "seq", None),
        P("dp", "seq", None),
        P("dp", "seq", None),
        P("dp", "seq"),
        P("dp", None, None),
        P(),
    )
    out_specs = (P("dp", "seq", None), P("dp", "seq", None), P("dp", "seq", None), P())
    return jax.shard_map(
        per_device, mesh=mesh, in_specs=in_specs, out_specs=out_specs, check_vma=False
    )
```

profile of v0, /device:TPU:4, one launch (start us, length us, event | category | flops | bytes accessed | tf_op | source)
XLA Modules:
  0.0 903.5 jit_solution(13056101979047803530)
XLA Ops:
  9.3 15.2 %all-to-all-start = ((bf16[128,16,128]{0,2,1:T(8,128)(2,1)}), bf16[128,16,128]{0,2,1:T(8,128)(2,1)S(1)}, u32[]{:S(2)}, u32[]{:S(2)}) async-start(bf16[128,16,128]{0,2,1:T(8,128)(2,1)} %bitcast.18), calls=%async_computation | async-start | bytes 1048576 | tf_op jit(solution)/shard_map/all_to_all | solution.py:151
  26.8 3.8 collective-permute-start
  31.7 52.5 %all_gather.3 = s32[1,2048]{1,0:T(1,128)S(1)} all-gather(s32[1,128]{1,0:T(1,128)S(1)} %copy-done.122), channel_id=1, replica_groups=mesh['dp'=32,'seq'=16] {'seq'}, dimensions={1}, use_global_device_ids=true | all-gather | bytes 8704 | tf_op jit(solution)/shard_map/all_gather | solution.py:142
  87.2 8.8 all-to-all-start.1
  101.4 16.4 %all-to-all-done.1 = bf16[128,16,128]{0,2,1:T(8,128)(2,1)S(1)} async-done(((bf16[128,16,128]{0,2,1:T(8,128)(2,1)}), bf16[128,16,128]{0,2,1:T(8,128)(2,1)S(1)}, u32[]{:S(2)}, u32[]{:S(2)}) %all-to-all-start.1) | async-done | bytes 524320 | tf_op jit(solution)/shard_map/all_to_all | solution.py:152
  117.8 7.0 all-to-all-start.2
  124.9 40.2 %fusion.322 = bf16[128,2048]{0,1:T(8,128)(2,1)S(1)} fusion(bf16[128,2048]{0,1:T(8,128)(2,1)S(1)} %bitcast.375, f32[2048]{0:T(1024)S(1)} %bitcast.429, f32[2048]{0:T(1024)S(1)} %bitcast.431, f32[2048]{0:T(1024)S(1)} %bitcast.435, f32[2048]{0:T(1024)S(1)} %bitcast.437, f32[2048]{0:T(1024)S(1)} %bitcast.439, f32[2048]{0:T(1024)S(1)} %bitcast.441, ...), kind=kLoop, calls=%fused_computation.710 | loop fusion | flops 116391936 | bytes 1838976 | tf_op jit(solution)/shard_map/convert_element_type | solution.py:149
  166.1 12.0 %all-to-all-start.3 = ((bf16[128,16,128]{2,0,1:T(8,128)(2,1)}), bf16[128,16,128]{2,0,1:T(8,128)(2,1)S(1)}, u32[]{:S(2)}, u32[]{:S(2)}) async-start(bf16[128,16,128]{2,0,1:T(8,128)(2,1)} %copy.195), calls=%async_computation.3 | async-start | bytes 1048576 | tf_op jit(solution)/shard_map/all_to_all | solution.py:153
  185.8 17.3 %all-to-all-done.3 = bf16[128,16,128]{2,0,1:T(8,128)(2,1)S(1)} async-done(((bf16[128,16,128]{2,0,1:T(8,128)(2,1)}), bf16[128,16,128]{2,0,1:T(8,128)(2,1)S(1)}, u32[]{:S(2)}, u32[]{:S(2)}) %all-to-all-start.3) | async-done | bytes 524320 | tf_op jit(solution)/shard_map/all_to_all | solution.py:153
  204.6 67.1 %while.18 = (s32[]{:T(128)}, bf16[2,2048,64]{1,2,0:T(8,128)(2,1)}, bf16[2,2048,64]{1,2,0:T(8,128)(2,1)}, bf16[2,2048,64]{1,2,0:T(8,128)(2,1)}, pred[16,4]{1,0:T(...) while((s32[]{:T(128)}, bf16[2,2048,64]{1,2,0:T(8,128)(2,1)}, ...), condition=%wide.region_6.7_spmd, body=%wide.region_1.6_spmd.sunk | while | flops 1074403328 | bytes 83230208 | solution.py:126
  207.2 4.9 fusion.503
  240.7 4.9 fusion.503
  265.4 3.1 fusion.509
  273.9 6.5 all-to-all-start.4
  282.8 24.3 %all-to-all-done.4 = bf16[16,128,128]{1,2,0:T(8,128)(2,1)S(1)} async-done(((bf16[16,128,128]{1,2,0:T(8,128)(2,1)}), bf16[16,128,128]{1,2,0:T(8,128)(2,1)S(1)}, u32[]{:S(2)}, u32[]{:S(2)}) %all-to-all-start.4) | async-done | bytes 524320 | tf_op jit(solution)/shard_map/all_to_all | solution.py:160
  307.1 16.3 %all-to-all-start.5 = ((bf16[16,128,128]{2,1,0:T(8,128)(2,1)}), bf16[16,128,128]{2,1,0:T(8,128)(2,1)S(1)}, u32[]{:S(2)}, u32[]{:S(2)}) async-start(bf16[16,128,128]{2,1,0:T(8,128)(2,1)} %copy.199), calls=%async_computation.5 | async-start | bytes 1048576 | tf_op jit(solution)/shard_map/all_to_all | solution.py:161
  324.8 25.9 %all-to-all-done.5 = bf16[16,128,128]{2,1,0:T(8,128)(2,1)S(1)} async-done(((bf16[16,128,128]{2,1,0:T(8,128)(2,1)}), bf16[16,128,128]{2,1,0:T(8,128)(2,1)S(1)}, u32[]{:S(2)}, u32[]{:S(2)}) %all-to-all-start.5) | async-done | bytes 524320 | tf_op jit(solution)/shard_map/all_to_all | solution.py:161
  350.7 7.0 all-to-all-start.6
  360.8 25.3 %all-to-all-done.6 = bf16[16,128,128]{2,1,0:T(8,128)(2,1)S(1)} async-done(((bf16[16,128,128]{2,1,0:T(8,128)(2,1)}), bf16[16,128,128]{2,1,0:T(8,128)(2,1)S(1)}, u32[]{:S(2)}, u32[]{:S(2)}) %all-to-all-start.6) | async-done | bytes 524320 | tf_op jit(solution)/shard_map/all_to_all | solution.py:162
  387.8 3.4 fusion.321
  391.3 3.6 fusion.223
  395.0 4.1 fusion.235
  399.1 3.6 fusion.247
  402.8 3.6 fusion.259
  406.4 3.6 fusion.271
  410.0 3.8 fusion.283
  414.2 4.2 fusion.295
  418.5 4.3 fusion.307
  422.7 4.2 fusion.319
  429.7 5.8 stack.259
  435.9 41.2 %fusion.447 = bf16[1,128,2048]{1,2,0:T(8,128)(2,1)S(1)} fusion(f32[2048]{0:T(1024)S(1)} %bitcast.430, bf16[63,2048]{0,1:T(8,128)(2,1)S(1)} %collective-permute-done.1, bf16[128,2048]{0,1:T(8,128)(2,1)S(1)} %bitcast.391, pred[128]{0:T(512)(128)(4,1)S(1)} %get-tuple-element.460, f32[2048]{0:T(1024)S(1)} %bitcast.432, ...), kind=kLoop, calls=%fused_computation.838 | loop fusion | flops 116391936 | bytes 1838976 | tf_op jit(solution)/shard_map/broadcast_in_dim | solution.py:169
  478.1 416.2 %all-reduce.2.cloned.1.call-done = f32[64,2048]{1,0:T(8,128)} async-done(((f32[64,2048]{1,0:T(8,128)}), f32[64,2048]{1,0:T(8,128)}) %all-reduce.2.cloned.1.call-update) | async-done | bytes 524304 | tf_op jit(solution)/shard_map/psum | solution.py:168
  (382 shorter events, 93.2 us)
Async XLA Ops:
  9.3 77.8 %all-to-all-start = ((bf16[128,16,128]{0,2,1:T(8,128)(2,1)}), bf16[128,16,128]{0,2,1:T(8,128)(2,1)S(1)}, u32[]{:S(2)}, u32[]{:S(2)}) async-start(bf16[128,16,128]{0,2,1:T(8,128)(2,1)} %bitcast.18), calls=%async_computation | async-start | bytes 1048576 | tf_op jit(solution)/shard_map/all_to_all | solution.py:151
  26.8 98.0 %collective-permute-start = (bf16[63,2048]{0,1:T(8,128)(2,1)}, bf16[63,2048]{0,1:T(8,128)(2,1)S(1)}, u32[]{:S(2)}, u32[]{:S(2)}) collective-permute-start(bf16[63,2048]{0,1:T(8,128)(2,1)} %slice_bitcast_fusion), channel_id=1, source_target_pairs={{0,1},{1,2},{2,3},{3,4},{4,5},{5,6},{6,7},{7,8},{8,9},{9,10},{10,1... | collective-permute-start | bytes 774152 | tf_op jit(solution)/shard_map/ppermute | solution.py:13
  87.2 91.0 %copy-start.2 = (s32[1,16,4]{1,2,0:T(4,128)S(1)}, s32[1,16,4]{1,2,0:T(4,128)}, u32[]{:S(2)}) copy-start(s32[1,16,4]{1,2,0:T(4,128)} %param.14) | copy-start | bytes 772
  87.2 30.6 %all-to-all-start.1 = ((bf16[128,16,128]{0,2,1:T(8,128)(2,1)}), bf16[128,16,128]{0,2,1:T(8,128)(2,1)S(1)}, u32[]{:S(2)}, u32[]{:S(2)}) async-start(bf16[128,16,128]{0,2,1:T(8,128)(2,1)} %bitcast.21), calls=%async_computation.1 | async-start | bytes 1048576 | tf_op jit(solution)/shard_map/all_to_all | solution.py:152
  97.1 85.8 %copy-start.30 = (f32[1,2048]{1,0:T(1,128)}, f32[1,2048]{1,0:T(1,128)S(1)}, u32[]{:S(2)}) copy-start(f32[1,2048]{1,0:T(1,128)S(1)} %get-tuple-element.351) | copy-start | bytes 24580
  97.1 85.8 %copy-start.32 = (f32[1,2048]{1,0:T(1,128)}, f32[1,2048]{1,0:T(1,128)S(1)}, u32[]{:S(2)}) copy-start(f32[1,2048]{1,0:T(1,128)S(1)} %get-tuple-element.352) | copy-start | bytes 24580
  97.1 85.8 %copy-start.34 = (f32[1,2048]{1,0:T(1,128)}, f32[1,2048]{1,0:T(1,128)S(1)}, u32[]{:S(2)}) copy-start(f32[1,2048]{1,0:T(1,128)S(1)} %get-tuple-element.353) | copy-start | bytes 24580
  97.1 85.8 %copy-start.36 = (f32[1,2048]{1,0:T(1,128)}, f32[1,2048]{1,0:T(1,128)S(1)}, u32[]{:S(2)}) copy-start(f32[1,2048]{1,0:T(1,128)S(1)} %get-tuple-element.354) | copy-start | bytes 24580
  97.1 85.8 %copy-start.38 = (f32[1,2048]{1,0:T(1,128)}, f32[1,2048]{1,0:T(1,128)S(1)}, u32[]{:S(2)}) copy-start(f32[1,2048]{1,0:T(1,128)S(1)} %get-tuple-element.355) | copy-start | bytes 24580
  97.1 85.8 %copy-start.40 = (f32[1,2048]{1,0:T(1,128)}, f32[1,2048]{1,0:T(1,128)S(1)}, u32[]{:S(2)}) copy-start(f32[1,2048]{1,0:T(1,128)S(1)} %get-tuple-element.356) | copy-start | bytes 24580
  97.1 85.8 %copy-start.42 = (f32[1,2048]{1,0:T(1,128)}, f32[1,2048]{1,0:T(1,128)S(1)}, u32[]{:S(2)}) copy-start(f32[1,2048]{1,0:T(1,128)S(1)} %get-tuple-element.357) | copy-start | bytes 24580
  97.1 85.8 %copy-start.44 = (f32[1,2048]{1,0:T(1,128)}, f32[1,2048]{1,0:T(1,128)S(1)}, u32[]{:S(2)}) copy-start(f32[1,2048]{1,0:T(1,128)S(1)} %get-tuple-element.358) | copy-start | bytes 24580
  97.1 85.8 %copy-start.46 = (f32[1,2048]{1,0:T(1,128)}, f32[1,2048]{1,0:T(1,128)S(1)}, u32[]{:S(2)}) copy-start(f32[1,2048]{1,0:T(1,128)S(1)} %get-tuple-element.359) | copy-start | bytes 24580
  97.1 85.8 %copy-start.48 = (f32[1,2048]{1,0:T(1,128)}, f32[1,2048]{1,0:T(1,128)S(1)}, u32[]{:S(2)}) copy-start(f32[1,2048]{1,0:T(1,128)S(1)} %get-tuple-element.360) | copy-start | bytes 24580
  97.2 85.8 %copy-start.50 = (f32[1,2048]{1,0:T(1,128)}, f32[1,2048]{1,0:T(1,128)S(1)}, u32[]{:S(2)}) copy-start(f32[1,2048]{1,0:T(1,128)S(1)} %get-tuple-element.361) | copy-start | bytes 24580
  97.2 85.8 %copy-start.52 = (f32[1,2048]{1,0:T(1,128)}, f32[1,2048]{1,0:T(1,128)S(1)}, u32[]{:S(2)}) copy-start(f32[1,2048]{1,0:T(1,128)S(1)} %get-tuple-element.362) | copy-start | bytes 24580
  97.2 85.8 %copy-start.54 = (f32[1,2048]{1,0:T(1,128)}, f32[1,2048]{1,0:T(1,128)S(1)}, u32[]{:S(2)}) copy-start(f32[1,2048]{1,0:T(1,128)S(1)} %get-tuple-element.363) | copy-start | bytes 24580
  97.2 85.8 %copy-start.56 = (f32[1,2048]{1,0:T(1,128)}, f32[1,2048]{1,0:T(1,128)S(1)}, u32[]{:S(2)}) copy-start(f32[1,2048]{1,0:T(1,128)S(1)} %get-tuple-element.364) | copy-start | bytes 24580
  97.2 85.8 %copy-start.58 = (f32[1,2048]{1,0:T(1,128)}, f32[1,2048]{1,0:T(1,128)S(1)}, u32[]{:S(2)}) copy-start(f32[1,2048]{1,0:T(1,128)S(1)} %get-tuple-element.365) | copy-start | bytes 24580
  117.8 48.3 %all-to-all-start.2 = ((bf16[128,16,128]{0,2,1:T(8,128)(2,1)}), bf16[128,16,128]{0,2,1:T(8,128)(2,1)S(1)}, u32[]{:S(2)}, u32[]{:S(2)}) async-start(bf16[128,16,128]{0,2,1:T(8,128)(2,1)} %bitcast.24), calls=%async_computation.2 | async-start | bytes 1048576 | tf_op jit(solution)/shard_map/all_to_all | solution.py:154
  166.1 37.0 %all-to-all-start.3 = ((bf16[128,16,128]{2,0,1:T(8,128)(2,1)}), bf16[128,16,128]{2,0,1:T(8,128)(2,1)S(1)}, u32[]{:S(2)}, u32[]{:S(2)}) async-start(bf16[128,16,128]{2,0,1:T(8,128)(2,1)} %copy.195), calls=%async_computation.3 | async-start | bytes 1048576 | tf_op jit(solution)/shard_map/all_to_all | solution.py:153
  273.9 33.2 %all-to-all-start.4 = ((bf16[16,128,128]{1,2,0:T(8,128)(2,1)}), bf16[16,128,128]{1,2,0:T(8,128)(2,1)S(1)}, u32[]{:S(2)}, u32[]{:S(2)}) async-start(bf16[16,128,128]{1,2,0:T(8,128)(2,1)} %copy.198), calls=%async_computation.4 | async-start | bytes 1048576 | tf_op jit(solution)/shard_map/all_to_all | solution.py:160
  282.8 105.0 %copy-start.99 = (pred[128]{0:T(512)(128)(4,1)S(1)}, pred[128]{0:T(512)(128)(4,1)}, u32[]{:S(2)}) copy-start(pred[128]{0:T(512)(128)(4,1)} %get-tuple-element.523) | copy-start | bytes 388
  282.8 105.0 %copy-start.102 = (pred[128]{0:T(512)(128)(4,1)S(1)}, pred[128]{0:T(512)(128)(4,1)}, u32[]{:S(2)}) copy-start(pred[128]{0:T(512)(128)(4,1)} %get-tuple-element.461) | copy-start | bytes 388
  282.8 105.0 %copy-start.103 = (pred[128]{0:T(512)(128)(4,1)S(1)}, pred[128]{0:T(512)(128)(4,1)}, u32[]{:S(2)}) copy-start(pred[128]{0:T(512)(128)(4,1)} %get-tuple-element.470) | copy-start | bytes 388
  282.8 105.0 %copy-start.104 = (pred[128]{0:T(512)(128)(4,1)S(1)}, pred[128]{0:T(512)(128)(4,1)}, u32[]{:S(2)}) copy-start(pred[128]{0:T(512)(128)(4,1)} %get-tuple-element.479) | copy-start | bytes 388
  282.8 105.0 %copy-start.105 = (pred[128]{0:T(512)(128)(4,1)S(1)}, pred[128]{0:T(512)(128)(4,1)}, u32[]{:S(2)}) copy-start(pred[128]{0:T(512)(128)(4,1)} %get-tuple-element.488) | copy-start | bytes 388
  282.8 105.0 %copy-start.121 = (pred[128]{0:T(512)(128)(4,1)S(1)}, pred[128]{0:T(512)(128)(4,1)}, u32[]{:S(2)}) copy-start(pred[128]{0:T(512)(128)(4,1)} %get-tuple-element.497) | copy-start | bytes 388
  307.1 43.6 %all-to-all-start.5 = ((bf16[16,128,128]{2,1,0:T(8,128)(2,1)}), bf16[16,128,128]{2,1,0:T(8,128)(2,1)S(1)}, u32[]{:S(2)}, u32[]{:S(2)}) async-start(bf16[16,128,128]{2,1,0:T(8,128)(2,1)} %copy.199), calls=%async_computation.5 | async-start | bytes 1048576 | tf_op jit(solution)/shard_map/all_to_all | solution.py:161
  350.7 35.4 %all-to-all-start.6 = ((bf16[16,128,128]{2,1,0:T(8,128)(2,1)}), bf16[16,128,128]{2,1,0:T(8,128)(2,1)S(1)}, u32[]{:S(2)}, u32[]{:S(2)}) async-start(bf16[16,128,128]{2,1,0:T(8,128)(2,1)} %copy.201), calls=%async_computation.6 | async-start | bytes 1048576 | tf_op jit(solution)/shard_map/all_to_all | solution.py:162
  357.7 536.6 %all-reduce.2.cloned.1.call-start = ((), (), s32[]{:S(2)}) async-start(), calls=%async_computation.7 | async-start | bytes 1048576 | tf_op jit(solution)/shard_map/psum | solution.py:168
  386.4 49.1 %collective-permute-start.1 = (bf16[63,2048]{0,1:T(8,128)(2,1)S(1)}, bf16[63,2048]{0,1:T(8,128)(2,1)S(1)}, u32[]{:S(2)}, u32[]{:S(2)}) collective-permute-start(bf16[63,2048]{0,1:T(8,128)(2,1)S(1)} %bitcast.390), channel_id=1, source_target_pairs={{1,0},{2,1},{3,2},{4,3},{5,4},{6,5},{7,6},{8,7},{9,8},{10,9},{11,1... | collective-permute-start | bytes 774152 | tf_op jit(solution)/shard_map/ppermute | solution.py:13
  (105 other events, 4078.8 us)
Sparse Core Ops, SparseCore 0:
  435.6 458.6 all-reduce.1
where the time goes:
time: 913 us; the launch traced here: 903 us
  waiting for transfers between devices  525 us (58%)
  other arithmetic  143 us (16%)
  starting transfers between devices  78.1 us (9%)
  blocking collectives  52.5 us (6%)
  local copies, waits for them, and re-layouts  51.7 us (6%)
  matrix products  35.5 us (4%)
  between operations  16.6 us (2%)
    psum x1, waiting for transfers between devices, per_device(): f_grad = lax.psum(f_local, ('dp', 'seq')) / shards  416 us
    all_gather x1, blocking collectives, per_device(): all_ids = lax.all_gather(segment_ids, 'seq', axis=1, tiled=True)[0]  52.5 us
    broadcast_in_dim x1, other arithmetic, per_device(): return (q_back[None], k_back[None], e_grad[None], f_grad)  41.2 us
    reduce_sum x11, other arithmetic, tap_gradient(): sums.append(jnp.sum(jnp.where(match, piece * grad_wide, 0.0), axis=0))  41 us
    convert_element_type x1, other arithmetic, per_device(): causal_conv(padded, left_ids, conv_weight, rows).astype(jnp.bfloat16)  40.2 us
    dot_general x16, matrix products, contract(): return jnp.einsum(form, left, right, preferred_element_type=jnp.float32)  26.3 us
    all_to_all x1, waiting for transfers between devices, per_device(): lax.all_to_all(k_grad, 'seq', split_axis=0, concat_axis=1, tiled=True)  25.9 us
    all_to_all x1, waiting for transfers between devices, per_device(): lax.all_to_all(v_grad, 'seq', split_axis=0, concat_axis=1, tiled=True)  25.3 us
  transfers between devices with their start and end apart: 10, of which 6 were waited for; matrix products, arithmetic and copies ran while one was open for 17% of the time, Pallas kernels for 0%

commit v1 on v0

--- a/solution.py
+++ b/solution.py
@@ -165,7 +165,7 @@
     after = jnp.concatenate([v_back, later], axis=0)
     e_grad = anti_conv(after, right_ids, conv_weight, rows).astype(jnp.bfloat16)
     f_local = tap_gradient(v_back, padded, left_ids, taps)
-    f_grad = lax.psum(f_local, ("dp", "seq")) / shards
+    f_grad = lax.psum(lax.psum(f_local, "dp"), "seq") / shards
     return (q_back[None], k_back[None], e_grad[None], f_grad)
 
 

time: 913 us -> 683 us (0.75)
  the two profiles are of different devices: /device:TPU:4 before, /device:TPU:2 now
where the time goes in v1:
time: 683 us; the launch traced here: 673 us
  waiting for transfers between devices  287 us (42%)
  other arithmetic  149 us (22%)
  starting transfers between devices  75.5 us (11%)
  local copies, waits for them, and re-layouts  56.5 us (8%)
  blocking collectives  52.5 us (8%)
  matrix products  35.5 us (5%)
  between operations  16.1 us (2%)
    psum x2, waiting for transfers between devices, per_device(): f_grad = lax.psum(lax.psum(f_local, 'dp'), 'seq') / shards  231 us
    all_gather x1, blocking collectives, per_device(): all_ids = lax.all_gather(segment_ids, 'seq', axis=1, tiled=True)[0]  52.5 us
    reduce_sum x11, other arithmetic, tap_gradient(): sums.append(jnp.sum(jnp.where(match, piece * grad_wide, 0.0), axis=0))  46.4 us
    convert_element_type x1, other arithmetic, per_device(): causal_conv(padded, left_ids, conv_weight, rows).astype(jnp.bfloat16)  40.2 us
    broadcast_in_dim x1, other arithmetic, per_device(): return (q_back[None], k_back[None], e_grad[None], f_grad)  39.2 us
    dot_general x16, matrix products, contract(): return jnp.einsum(form, left, right, preferred_element_type=jnp.float32)  26.3 us
    all_to_all x1, waiting for transfers between devices, per_device(): lax.all_to_all(v_grad, 'seq', split_axis=0, concat_axis=1, tiled=True)  19.6 us
    all_to_all x1, waiting for transfers between devices, per_device(): lax.all_to_all(values, 'seq', split_axis=1, concat_axis=0, tiled=True)  18.5 us
  transfers between devices with their start and end apart: 11, of which 5 were waited for; matrix products, arithmetic and copies ran while one was open for 25% of the time, Pallas kernels for 0%

profile of v1, /device:TPU:2, one launch (start us, length us, event | category | flops | bytes accessed | tf_op | source)
XLA Modules:
  0.0 672.7 jit_solution(16653437469785163637)
XLA Ops:
  9.4 15.2 %all-to-all-start = ((bf16[128,16,128]{0,2,1:T(8,128)(2,1)}), bf16[128,16,128]{0,2,1:T(8,128)(2,1)S(1)}, u32[]{:S(2)}, u32[]{:S(2)}) async-start(bf16[128,16,128]{0,2,1:T(8,128)(2,1)} %bitcast.18), calls=%async_computation | async-start | bytes 1048576 | tf_op jit(solution)/shard_map/all_to_all | solution.py:151
  26.9 3.8 collective-permute-start
  31.8 52.5 %all_gather.3 = s32[1,2048]{1,0:T(1,128)S(1)} all-gather(s32[1,128]{1,0:T(1,128)S(1)} %copy-done.126), channel_id=1, replica_groups=mesh['dp'=32,'seq'=16] {'seq'}, dimensions={1}, use_global_device_ids=true | all-gather | bytes 8704 | tf_op jit(solution)/shard_map/all_gather | solution.py:142
  87.2 8.8 %all-to-all-start.1 = ((bf16[128,16,128]{0,2,1:T(8,128)(2,1)}), bf16[128,16,128]{0,2,1:T(8,128)(2,1)S(1)}, u32[]{:S(2)}, u32[]{:S(2)}) async-start(bf16[128,16,128]{0,2,1:T(8,128)(2,1)} %bitcast.21), calls=%async_computation.1 | async-start | bytes 1048576 | tf_op jit(solution)/shard_map/all_to_all | solution.py:152
  100.4 17.5 %all-to-all-done.1 = bf16[128,16,128]{0,2,1:T(8,128)(2,1)S(1)} async-done(((bf16[128,16,128]{0,2,1:T(8,128)(2,1)}), bf16[128,16,128]{0,2,1:T(8,128)(2,1)S(1)}, u32[]{:S(2)}, u32[]{:S(2)}) %all-to-all-start.1) | async-done | bytes 524320 | tf_op jit(solution)/shard_map/all_to_all | solution.py:152
  117.9 7.0 %all-to-all-start.2 = ((bf16[128,16,128]{0,2,1:T(8,128)(2,1)}), bf16[128,16,128]{0,2,1:T(8,128)(2,1)S(1)}, u32[]{:S(2)}, u32[]{:S(2)}) async-start(bf16[128,16,128]{0,2,1:T(8,128)(2,1)} %bitcast.24), calls=%async_computation.2 | async-start | bytes 1048576 | tf_op jit(solution)/shard_map/all_to_all | solution.py:154
  124.9 40.2 %fusion.322 = bf16[128,2048]{0,1:T(8,128)(2,1)S(1)} fusion(bf16[128,2048]{0,1:T(8,128)(2,1)S(1)} %bitcast.375, f32[2048]{0:T(1024)S(1)} %bitcast.429, f32[2048]{0:T(1024)S(1)} %bitcast.431, f32[2048]{0:T(1024)S(1)} %bitcast.435, f32[2048]{0:T(1024)S(1)} %bitcast.437, f32[2048]{0:T(1024)S(1)} %bitcast.439, f32[2048]{0:T(1024)S(1)} %bitcast.441, ...), kind=kLoop, calls=%fused_computation.710 | loop fusion | flops 116391936 | bytes 1838976 | tf_op jit(solution)/shard_map/convert_element_type | solution.py:149
  166.2 12.0 %all-to-all-start.3 = ((bf16[128,16,128]{2,0,1:T(8,128)(2,1)}), bf16[128,16,128]{2,0,1:T(8,128)(2,1)S(1)}, u32[]{:S(2)}, u32[]{:S(2)}) async-start(bf16[128,16,128]{2,0,1:T(8,128)(2,1)} %copy.195), calls=%async_computation.3 | async-start | bytes 1048576 | tf_op jit(solution)/shard_map/all_to_all | solution.py:153
  184.7 18.5 %all-to-all-done.3 = bf16[128,16,128]{2,0,1:T(8,128)(2,1)S(1)} async-done(((bf16[128,16,128]{2,0,1:T(8,128)(2,1)}), bf16[128,16,128]{2,0,1:T(8,128)(2,1)S(1)}, u32[]{:S(2)}, u32[]{:S(2)}) %all-to-all-start.3) | async-done | bytes 524320 | tf_op jit(solution)/shard_map/all_to_all | solution.py:153
  204.7 67.1 %while.18 = (s32[]{:T(128)}, bf16[2,2048,64]{1,2,0:T(8,128)(2,1)}, bf16[2,2048,64]{1,2,0:T(8,128)(2,1)}, bf16[2,2048,64]{1,2,0:T(8,128)(2,1)}, pred[16,4]{1,0:T(...) while((s32[]{:T(128)}, bf16[2,2048,64]{1,2,0:T(8,128)(2,1)}, ...), condition=%wide.region_6.7_spmd, body=%wide.region_1.6_spmd.sunk | while | flops 1074403328 | bytes 83230208 | solution.py:126
  207.2 4.9 fusion.503
  231.9 3.1 fusion.509
  240.7 4.9 fusion.503
  265.4 3.1 fusion.509
  274.3 6.9 %all-to-all-start.6 = ((bf16[16,128,128]{2,1,0:T(8,128)(2,1)}), bf16[16,128,128]{2,1,0:T(8,128)(2,1)S(1)}, u32[]{:S(2)}, u32[]{:S(2)}) async-start(bf16[16,128,128]{2,1,0:T(8,128)(2,1)} %copy.201), calls=%async_computation.6 | async-start | bytes 1048576 | tf_op jit(solution)/shard_map/all_to_all | solution.py:162
  288.2 19.6 %all-to-all-done.6 = bf16[16,128,128]{2,1,0:T(8,128)(2,1)S(1)} async-done(((bf16[16,128,128]{2,1,0:T(8,128)(2,1)}), bf16[16,128,128]{2,1,0:T(8,128)(2,1)S(1)}, u32[]{:S(2)}, u32[]{:S(2)}) %all-to-all-start.6) | async-done | bytes 524320 | tf_op jit(solution)/shard_map/all_to_all | solution.py:162
  307.8 7.1 %all-to-all-start.4 = ((bf16[16,128,128]{1,2,0:T(8,128)(2,1)}), bf16[16,128,128]{1,2,0:T(8,128)(2,1)S(1)}, u32[]{:S(2)}, u32[]{:S(2)}) async-start(bf16[16,128,128]{1,2,0:T(8,128)(2,1)} %copy.198), calls=%async_computation.4 | async-start | bytes 1048576 | tf_op jit(solution)/shard_map/all_to_all | solution.py:160
  316.6 4.2 fusion.223
  320.9 4.8 fusion.235
  325.7 4.0 fusion.321
  329.8 4.2 fusion.247
  334.1 4.2 fusion.259
  338.3 4.2 fusion.271
  342.6 4.4 fusion.283
  346.9 13.2 %all-to-all-start.5 = ((bf16[16,128,128]{2,1,0:T(8,128)(2,1)}), bf16[16,128,128]{2,1,0:T(8,128)(2,1)S(1)}, u32[]{:S(2)}, u32[]{:S(2)}) async-start(bf16[16,128,128]{2,1,0:T(8,128)(2,1)} %copy.199), calls=%async_computation.5 | async-start | bytes 1048576 | tf_op jit(solution)/shard_map/all_to_all | solution.py:161
  362.9 4.2 fusion.295
  367.4 4.9 fusion.307
  372.2 4.8 fusion.319
  377.1 12.3 %stack.259 = f32[64,2048]{1,0:T(8,128)} concatenate(f32[1,2048]{1,0:T(1,128)} %bitcast.592, f32[1,2048]{1,0:T(1,128)} %bitcast.560, f32[1,2048]{1,0:T(1,128)} %bitcast.561, f32[1,2048]{1,0:T(1,128)} %bitcast.562, f32[1,2048]{1,0:T(1,128)} %bitcast.563, f32[1,2048]{1,0:T(1,128)} %bitcast.564, f32[1,2048]{1,0:T(1,128)} %bitcast.591, f32[1,2048]{1,0:T(1,128)} %bitcast.590, ...), dimensions={0} | concatenate | bytes 1048576 | tf_op jit(solution)/shard_map/stack | solution.py:57
  391.9 132.6 %all-reduce.3.cloned.1.call-done = f32[64,2048]{1,0:T(8,128)} async-done(((f32[64,2048]{1,0:T(8,128)}), f32[64,2048]{1,0:T(8,128)}) %all-reduce.3.cloned.1.call-update) | async-done | bytes 524304 | tf_op jit(solution)/shard_map/psum | solution.py:168
  524.9 39.2 %fusion.447 = bf16[1,128,2048]{1,2,0:T(8,128)(2,1)S(1)} fusion(f32[2048]{0:T(1024)S(1)} %bitcast.430, bf16[63,2048]{0,1:T(8,128)(2,1)S(1)} %collective-permute-done.1, bf16[128,2048]{0,1:T(8,128)(2,1)S(1)} %bitcast.391, pred[128]{0:T(512)(128)(4,1)} %get-tuple-element.460, f32[2048]{0:T(1024)S(1)} %bitcast.432, pred[128]{0:T(512)(128)(4,1)} %get-tuple-element.399, ...), kind=kLoop, calls=%fused_computation.838 | loop fusion | flops 116391936 | bytes 1838976 | tf_op jit(solution)/shard_map/broadcast_in_dim | solution.py:169
  565.1 98.6 %all-reduce.5.cloned.1.call-done = f32[64,2048]{1,0:T(8,128)} async-done(((f32[64,2048]{1,0:T(8,128)}), f32[64,2048]{1,0:T(8,128)}) %all-reduce.5.cloned.1.call-update) | async-done | bytes 524304 | tf_op jit(solution)/shard_map/psum | solution.py:168
  (393 shorter events, 91.0 us)
Async XLA Ops:
  9.4 77.9 %all-to-all-start = ((bf16[128,16,128]{0,2,1:T(8,128)(2,1)}), bf16[128,16,128]{0,2,1:T(8,128)(2,1)S(1)}, u32[]{:S(2)}, u32[]{:S(2)}) async-start(bf16[128,16,128]{0,2,1:T(8,128)(2,1)} %bitcast.18), calls=%async_computation | async-start | bytes 1048576 | tf_op jit(solution)/shard_map/all_to_all | solution.py:151
  26.9 98.0 %collective-permute-start = (bf16[63,2048]{0,1:T(8,128)(2,1)}, bf16[63,2048]{0,1:T(8,128)(2,1)S(1)}, u32[]{:S(2)}, u32[]{:S(2)}) collective-permute-start(bf16[63,2048]{0,1:T(8,128)(2,1)} %slice_bitcast_fusion), channel_id=1, source_target_pairs={{0,1},{1,2},{2,3},{3,4},{4,5},{5,6},{6,7},{7,8},{8,9},{9,10},{10,1... | collective-permute-start | bytes 774152 | tf_op jit(solution)/shard_map/ppermute | solution.py:13
  87.2 30.6 %all-to-all-start.1 = ((bf16[128,16,128]{0,2,1:T(8,128)(2,1)}), bf16[128,16,128]{0,2,1:T(8,128)(2,1)S(1)}, u32[]{:S(2)}, u32[]{:S(2)}) async-start(bf16[128,16,128]{0,2,1:T(8,128)(2,1)} %bitcast.21), calls=%async_computation.1 | async-start | bytes 1048576 | tf_op jit(solution)/shard_map/all_to_all | solution.py:152
  117.9 48.3 %all-to-all-start.2 = ((bf16[128,16,128]{0,2,1:T(8,128)(2,1)}), bf16[128,16,128]{0,2,1:T(8,128)(2,1)S(1)}, u32[]{:S(2)}, u32[]{:S(2)}) async-start(bf16[128,16,128]{0,2,1:T(8,128)(2,1)} %bitcast.24), calls=%async_computation.2 | async-start | bytes 1048576 | tf_op jit(solution)/shard_map/all_to_all | solution.py:154
  166.2 37.0 %all-to-all-start.3 = ((bf16[128,16,128]{2,0,1:T(8,128)(2,1)}), bf16[128,16,128]{2,0,1:T(8,128)(2,1)S(1)}, u32[]{:S(2)}, u32[]{:S(2)}) async-start(bf16[128,16,128]{2,0,1:T(8,128)(2,1)} %copy.195), calls=%async_computation.3 | async-start | bytes 1048576 | tf_op jit(solution)/shard_map/all_to_all | solution.py:153
  274.3 33.6 %all-to-all-start.6 = ((bf16[16,128,128]{2,1,0:T(8,128)(2,1)}), bf16[16,128,128]{2,1,0:T(8,128)(2,1)S(1)}, u32[]{:S(2)}, u32[]{:S(2)}) async-start(bf16[16,128,128]{2,1,0:T(8,128)(2,1)} %copy.201), calls=%async_computation.6 | async-start | bytes 1048576 | tf_op jit(solution)/shard_map/all_to_all | solution.py:162
  307.8 39.1 %all-to-all-start.4 = ((bf16[16,128,128]{1,2,0:T(8,128)(2,1)}), bf16[16,128,128]{1,2,0:T(8,128)(2,1)S(1)}, u32[]{:S(2)}, u32[]{:S(2)}) async-start(bf16[16,128,128]{1,2,0:T(8,128)(2,1)} %copy.198), calls=%async_computation.4 | async-start | bytes 1048576 | tf_op jit(solution)/shard_map/all_to_all | solution.py:160
  315.3 209.3 %collective-permute-start.1 = (bf16[63,2048]{0,1:T(8,128)(2,1)S(1)}, bf16[63,2048]{0,1:T(8,128)(2,1)S(1)}, u32[]{:S(2)}, u32[]{:S(2)}) collective-permute-start(bf16[63,2048]{0,1:T(8,128)(2,1)S(1)} %bitcast.390), channel_id=1, source_target_pairs={{1,0},{2,1},{3,2},{4,3},{5,4},{6,5},{7,6},{8,7},{9,8},{10,9},{11,1... | collective-permute-start | bytes 774152 | tf_op jit(solution)/shard_map/ppermute | solution.py:13
  346.9 43.7 %all-to-all-start.5 = ((bf16[16,128,128]{2,1,0:T(8,128)(2,1)}), bf16[16,128,128]{2,1,0:T(8,128)(2,1)S(1)}, u32[]{:S(2)}, u32[]{:S(2)}) async-start(bf16[16,128,128]{2,1,0:T(8,128)(2,1)} %copy.199), calls=%async_computation.5 | async-start | bytes 1048576 | tf_op jit(solution)/shard_map/all_to_all | solution.py:161
  360.1 164.4 %all-reduce.3.cloned.1.call-start = ((), (), s32[]{:S(2)}) async-start(), calls=%async_computation.7 | async-start | bytes 1048576 | tf_op jit(solution)/shard_map/psum | solution.py:168
  367.1 157.5 %copy-start.20 = (f32[1,2048]{1,0:T(1,128)S(1)}, f32[1,2048]{1,0:T(1,128)}, u32[]{:S(2)}) copy-start(f32[1,2048]{1,0:T(1,128)} %copy-done.19) | copy-start | bytes 24580
  367.1 157.5 %copy-start.22 = (f32[1,2048]{1,0:T(1,128)S(1)}, f32[1,2048]{1,0:T(1,128)}, u32[]{:S(2)}) copy-start(f32[1,2048]{1,0:T(1,128)} %copy-done.21) | copy-start | bytes 24580
  367.1 157.5 %copy-start.24 = (f32[1,2048]{1,0:T(1,128)S(1)}, f32[1,2048]{1,0:T(1,128)}, u32[]{:S(2)}) copy-start(f32[1,2048]{1,0:T(1,128)} %copy-done.23) | copy-start | bytes 24580
  367.1 157.5 %copy-start.26 = (f32[1,2048]{1,0:T(1,128)S(1)}, f32[1,2048]{1,0:T(1,128)}, u32[]{:S(2)}) copy-start(f32[1,2048]{1,0:T(1,128)} %copy-done.25) | copy-start | bytes 24580
  367.1 157.5 %copy-start.28 = (f32[1,2048]{1,0:T(1,128)S(1)}, f32[1,2048]{1,0:T(1,128)}, u32[]{:S(2)}) copy-start(f32[1,2048]{1,0:T(1,128)} %copy-done.27) | copy-start | bytes 24580
  367.1 157.5 %copy-start.30 = (f32[1,2048]{1,0:T(1,128)S(1)}, f32[1,2048]{1,0:T(1,128)}, u32[]{:S(2)}) copy-start(f32[1,2048]{1,0:T(1,128)} %copy-done.29) | copy-start | bytes 24580
  367.1 157.5 %copy-start.32 = (f32[1,2048]{1,0:T(1,128)S(1)}, f32[1,2048]{1,0:T(1,128)}, u32[]{:S(2)}) copy-start(f32[1,2048]{1,0:T(1,128)} %copy-done.31) | copy-start | bytes 24580
  367.2 157.5 %copy-start.34 = (f32[1,2048]{1,0:T(1,128)S(1)}, f32[1,2048]{1,0:T(1,128)}, u32[]{:S(2)}) copy-start(f32[1,2048]{1,0:T(1,128)} %copy-done.33) | copy-start | bytes 24580
  367.2 157.5 %copy-start.36 = (f32[1,2048]{1,0:T(1,128)S(1)}, f32[1,2048]{1,0:T(1,128)}, u32[]{:S(2)}) copy-start(f32[1,2048]{1,0:T(1,128)} %copy-done.35) | copy-start | bytes 24580
  367.2 157.5 %copy-start.38 = (f32[1,2048]{1,0:T(1,128)S(1)}, f32[1,2048]{1,0:T(1,128)}, u32[]{:S(2)}) copy-start(f32[1,2048]{1,0:T(1,128)} %copy-done.37) | copy-start | bytes 24580
  367.2 157.5 %copy-start.40 = (f32[1,2048]{1,0:T(1,128)S(1)}, f32[1,2048]{1,0:T(1,128)}, u32[]{:S(2)}) copy-start(f32[1,2048]{1,0:T(1,128)} %copy-done.39) | copy-start | bytes 24580
  367.2 157.5 %copy-start.42 = (f32[1,2048]{1,0:T(1,128)S(1)}, f32[1,2048]{1,0:T(1,128)}, u32[]{:S(2)}) copy-start(f32[1,2048]{1,0:T(1,128)} %copy-done.41) | copy-start | bytes 24580
  367.2 157.5 %copy-start.44 = (f32[1,2048]{1,0:T(1,128)S(1)}, f32[1,2048]{1,0:T(1,128)}, u32[]{:S(2)}) copy-start(f32[1,2048]{1,0:T(1,128)} %copy-done.43) | copy-start | bytes 24580
  367.2 157.5 %copy-start.46 = (f32[1,2048]{1,0:T(1,128)S(1)}, f32[1,2048]{1,0:T(1,128)}, u32[]{:S(2)}) copy-start(f32[1,2048]{1,0:T(1,128)} %copy-done.45) | copy-start | bytes 24580
  367.2 157.5 %copy-start.48 = (f32[1,2048]{1,0:T(1,128)S(1)}, f32[1,2048]{1,0:T(1,128)}, u32[]{:S(2)}) copy-start(f32[1,2048]{1,0:T(1,128)} %copy-done.47) | copy-start | bytes 24580
  367.2 157.5 %copy-start.50 = (f32[1,2048]{1,0:T(1,128)S(1)}, f32[1,2048]{1,0:T(1,128)}, u32[]{:S(2)}) copy-start(f32[1,2048]{1,0:T(1,128)} %copy-done.49) | copy-start | bytes 24580
  367.2 157.5 %copy-start.52 = (f32[1,2048]{1,0:T(1,128)S(1)}, f32[1,2048]{1,0:T(1,128)}, u32[]{:S(2)}) copy-start(f32[1,2048]{1,0:T(1,128)} %copy-done.51) | copy-start | bytes 24580
  367.3 157.5 %copy-start.54 = (f32[1,2048]{1,0:T(1,128)S(1)}, f32[1,2048]{1,0:T(1,128)}, u32[]{:S(2)}) copy-start(f32[1,2048]{1,0:T(1,128)} %copy-done.53) | copy-start | bytes 24580
  367.3 157.5 %copy-start.56 = (f32[1,2048]{1,0:T(1,128)S(1)}, f32[1,2048]{1,0:T(1,128)}, u32[]{:S(2)}) copy-start(f32[1,2048]{1,0:T(1,128)} %copy-done.55) | copy-start | bytes 24580
  367.3 157.5 %copy-start.58 = (f32[1,2048]{1,0:T(1,128)S(1)}, f32[1,2048]{1,0:T(1,128)}, u32[]{:S(2)}) copy-start(f32[1,2048]{1,0:T(1,128)} %copy-done.57) | copy-start | bytes 24580
  367.3 157.5 %copy-start.60 = (f32[1,2048]{1,0:T(1,128)S(1)}, f32[1,2048]{1,0:T(1,128)}, u32[]{:S(2)}) copy-start(f32[1,2048]{1,0:T(1,128)} %copy-done.59) | copy-start | bytes 24580
  389.4 274.4 %all-reduce.5.cloned.1.call-start = ((), (), s32[]{:S(2)}) async-start(), calls=%async_computation.8 | async-start | bytes 1048576 | tf_op jit(solution)/shard_map/psum | solution.py:168
  (110 other events, 6943.1 us)
Sparse Core Ops, SparseCore 0:
  389.5 134.9 all-reduce.2
  526.9 136.7 all-reduce.4
